TPU v7x, 32 devices: a whole 2x2x4 slice. The times are simulated.
32 devices in a mesh: groups: 2 (over y), edge: 4 (over z), expert: 2 (over x), sys: 2 (over core).
Axes of the slice: x: 2, y: 2, z: 4, core: 2. Of those that a mesh axis runs over, the one named last changes fastest.
Arguments:
- edge_inputs: bfloat16 [8, 1792, 1280], P(('groups', 'expert', 'sys'), 'edge'), parts along dimension 0, may hold values from -6 to 6
- out_grad: bfloat16 [8, 1792, 1152], P(('groups', 'expert', 'sys'), 'edge'), parts along dimension 0, may hold values from -6 to 6
- expert_weights: bfloat16 [32, 1280, 1152], P('expert', 'edge'), may hold values from -0.15625 to 0.15625
- coef_table: float32 [16, 32], replicated, may hold values from 0.05 to 0.5
- system_kind: int32 [8], P('groups'), parts along dimension 0, may hold values from 0 to 15
- edge_counts: int32 [8], P('groups'), parts along dimension 0, may hold values from 896 to 1792, as said below
Outputs:
- input_grad: bfloat16 [8, 1792, 1280], P(('groups', 'expert', 'sys'), 'edge'), parts along dimension 0
- weight_grad: bfloat16 [64, 1280, 1152], P(('groups', 'expert'), 'edge'), parts along dimension 0
There are 2 independent parts, one for each index of `groups`. A program takes and returns all parts, laid end to end along the dimension named above; an argument that names none is the same for every part. Nothing has to cross between parts.
Inputs may be any that keep to these rules, and one draw needn't show every extreme that they name: `edge_counts`: the live edges of a system are its first ones. One system has all 1792 slots live and another exactly half of them.
All inputs are finite; a program needn't handle non-finite values.
Results may differ from a plain program's by a relative error of at most 0.018.
Values may be sent and summed in bfloat16 or wider, within the bound.
No kernel may reach another device: no remote copies, remote signals or barrier semaphores. Data moves between devices by JAX's collectives and lax.ppermute only.
A program may use at most 128 MiB of HBM per device.

v0:
```python
import math
import jax
import jax.numpy as jnp
from jax import lax
from jax.sharding import PartitionSpec as P


def body(edge_inputs, out_grad, expert_weights, coef_table, system_kind, edge_counts):
    highest = lax.Precision.HIGHEST
    edge_size = lax.axis_size("edge")
    expert_size = lax.axis_size("expert")
    sys_size = lax.axis_size("sys")
    edge_at = lax.axis_index("edge")
    expert_at = lax.axis_index("expert")
    sys_at = lax.axis_index("sys")
    systems = system_kind.shape[0]
    kinds = coef_table.shape[0]
    exp_local = expert_weights.shape[0]
    row_count = expert_weights.shape[1]
    width_out = expert_weights.shape[2]
    edge_rows = out_grad.shape[1]
    onehot = (system_kind[:, None] == jnp.arange(kinds, dtype=jnp.int32)[None, :]).astype(
        jnp.float32
    )
    coeffs = jnp.dot(onehot, coef_table, precision=highest)
    own_system = expert_at * sys_size + sys_at
    picked = jnp.arange(systems, dtype=jnp.int32) == own_system
    own_count = jnp.sum(jnp.where(picked, edge_counts, 0))
    positions = edge_at * edge_rows + jnp.arange(edge_rows, dtype=jnp.int32)
    masked_grad = jnp.where(
        (positions < own_count)[:, None], out_grad[0], jnp.zeros((), jnp.bfloat16)
    )
    features = edge_inputs[0]
    by_block = coeffs.reshape(expert_size, sys_size, -1)
    same_sys = lax.dynamic_slice_in_dim(by_block, sys_at, 1, 1)[:, 0, :]
    own_coeffs = lax.dynamic_slice_in_dim(same_sys, expert_at * exp_local, exp_local, 1)
    partials = jnp.sum(
        own_coeffs[:, :, None, None] * expert_weights.astype(jnp.float32)[None], axis=1
    ).astype(jnp.bfloat16)
    merged_rows = jnp.sum(
        lax.all_to_all(partials, "expert", split_axis=0, concat_axis=0, tiled=True).astype(
            jnp.float32
        ),
        axis=0,
    ).astype(jnp.bfloat16)
    product = lax.dot_general(
        masked_grad,
        lax.all_gather(merged_rows, "edge", axis=0, tiled=True),
        (((1,), (1,)), ((), ())),
        preferred_element_type=jnp.float32,
    )
    input_grad = product.astype(jnp.bfloat16)
    system_rows = lax.psum_scatter(
        lax.dot_general(
            features, masked_grad, (((0,), (0,)), ((), ())), preferred_element_type=jnp.float32
        ).astype(jnp.bfloat16),
        "edge",
        scatter_dimension=0,
        tiled=True,
    )
    local_coeffs = lax.dynamic_slice_in_dim(coeffs, expert_at * exp_local, exp_local, 1).T
    block_rows = lax.all_gather(system_rows[None], ("expert", "sys"), axis=0, tiled=True)
    span_rows = block_rows.shape[0]
    flat_rows = block_rows.reshape(span_rows, -1).astype(jnp.float32)
    folded = jnp.dot(local_coeffs, flat_rows, precision=highest)
    scale_factor = 1.0 / math.sqrt(edge_rows * edge_size)
    weight_grad = (
        (folded * scale_factor).reshape(exp_local, row_count, width_out).astype(jnp.bfloat16)
    )
    return (input_grad[None], weight_grad)


def solution(mesh):
    return jax.shard_map(
        body,
        mesh=mesh,
        in_specs=(
            P(("groups", "expert", "sys"), "edge", None),
            P(("groups", "expert", "sys"), "edge", None),
            P("expert", "edge", None),
            P(),
            P("groups"),
            P("groups"),
        ),
        out_specs=(
            P(("groups", "expert", "sys"), "edge", None),
            P(("groups", "expert"), "edge", None),
        ),
        check_vma=False,
    )
```

profile of v0, /device:TPU:0, one launch (start us, length us, event | category | flops | bytes accessed | tf_op | source)
XLA Modules:
  0.0 198.3 jit_solution(15670721173112743282)
XLA Ops:
  7.2 0.0 copy-start
  7.2 0.0 reduce-scatter.4.cloned.1.call-start
  7.2 1.4 fusion.13
  8.6 0.7 add_compare_fusion
  9.3 0.0 copy-done
  9.3 4.7 %fusion.1 = bf16[1280,1152]{0,1:T(8,128)(2,1)} fusion(bf16[1,448,1280]{2,1,0:T(8,128)(2,1)S(1)} %copy-done, bf16[1,448,1152]{2,1,0:T(8,128)(2,1)} %param.7, pred[448]{0:T(512)(128)(4,1)S(1)} %add_compare_fusion), kind=kOutput, calls=%fused_computation.4 | convolution fusion | flops 1323196416 | bytes 5128640 | tf_op jit(solution)/shard_map/dot_general | solution.py:54
  13.9 5.4 %copy.11 = bf16[1280,1152]{1,0:T(8,128)(2,1)} copy(bf16[1280,1152]{0,1:T(8,128)(2,1)} %fusion.1) | data formatting | bytes 5898240
  19.4 0.0 reduce-scatter.4.cloned.1.call-update
  19.4 0.0 all-gather.4.cloned.1.call-start
  19.5 0.0 copy-start.3
  19.5 0.0 copy-start.4
  19.5 13.6 %convert_element_type.25 = f32[16,320,1152]{2,1,0:T(8,128)} convert(bf16[16,320,1152]{2,1,0:T(8,128)(2,1)} %param.8) | non-fusion elementwise | flops 5898240 | bytes 35389440 | tf_op jit(solution)/shard_map/convert_element_type | solution.py:38
  33.1 0.0 copy-done.3
  33.1 0.0 copy-done.4
  33.1 0.2 fusion.11
  33.3 0.1 constant_dynamic-slice_fusion
  33.4 13.5 %multiply_reduce_fusion = bf16[2,320,1152]{2,1,0:T(8,128)(2,1)S(1)} fusion(f32[16,320,1152]{2,1,0:T(8,128)} %convert_element_type.25, f32[2,16]{1,0:T(2,128)S(1)} %bitcast.24), kind=kLoop, calls=%fused_computation.2 | loop fusion | flops 22855680 | bytes 25067648 | tf_op jit(solution)/shard_map/reduce_sum | solution.py:37
  46.8 0.0 copy-start.2
  46.9 22.3 %all_to_all.5 = bf16[2,320,1152]{2,1,0:T(8,128)(2,1)S(1)} all-to-all(bf16[2,320,1152]{2,1,0:T(8,128)(2,1)S(1)} %multiply_reduce_fusion), channel_id=1, replica_groups=mesh['groups'=2,'edge'=4,'expert'=2,'sys'=2] {'expert'}, dimensions={0} | all-to-all | bytes 2949120 | tf_op jit(solution)/shard_map/all_to_all | solution.py:41
  69.2 1.3 reduce_sum.32
  70.5 0.0 all-gather.4.cloned.1.call-update
  70.5 0.0 all-gather.6.cloned.1.call-start
  70.6 9.0 %reduce-scatter.4.cloned.1.call-done = bf16[320,1152]{1,0:T(8,128)(2,1)} async-done(((bf16[1280,1152]{1,0:T(8,128)(2,1)}), bf16[320,1152]{1,0:T(8,128)(2,1)}) %reduce-scatter.4.cloned.1.call-update) | async-done | bytes 737296 | tf_op jit(solution)/shard_map/reduce_scatter | solution.py:53
  79.6 0.0 all-gather.6.cloned.1.call-update
  79.7 62.1 %all-gather.4.cloned.1.call-done = bf16[1280,1152]{1,0:T(8,128)(2,1)} async-done(((bf16[320,1152]{1,0:T(8,128)(2,1)}), bf16[1280,1152]{1,0:T(8,128)(2,1)}) %all-gather.4.cloned.1.call-update) | async-done | bytes 2949136 | tf_op jit(solution)/shard_map/all_gather | solution.py:48
  141.8 0.0 copy-done.2
  141.8 4.6 %fusion.2 = bf16[1,448,1280]{2,1,0:T(8,128)(2,1)} fusion(bf16[1280,1152]{1,0:T(8,128)(2,1)} %all-gather.4.cloned.1.call-done, bf16[1,448,1152]{2,1,0:T(8,128)(2,1)S(1)} %copy-done.2, pred[448]{0:T(512)(128)(4,1)S(1)} %add_compare_fusion), kind=kOutput, calls=%fused_computation.6 | convolution fusion | flops 1322295296 | bytes 5128640 | tf_op jit(solution)/shard_map/dot_general | solution.py:46
  146.3 23.1 %all-gather.6.cloned.1.call-done = bf16[1280,1152]{1,0:T(8,128)(2,1)} async-done(((bf16[320,1152]{1,0:T(8,128)(2,1)}), bf16[1280,1152]{1,0:T(8,128)(2,1)}) %all-gather.6.cloned.1.call-update) | async-done | bytes 2949136 | tf_op jit(solution)/shard_map/all_gather | solution.py:62
  169.4 4.5 %reshape.31 = bf16[4,368640]{1,0:T(4,128)(2,1)} reshape(bf16[1280,1152]{1,0:T(8,128)(2,1)} %all-gather.6.cloned.1.call-done) | data formatting | bytes 5898240 | tf_op jit(solution)/shard_map/reshape | solution.py:64
  173.9 12.6 %fusion = bf16[16,368640]{1,0:T(8,128)(2,1)S(1)} fusion(bf16[4,368640]{1,0:T(4,128)(2,1)} %reshape.31, f32[4,32]{1,0:T(4,128)S(1)} %fusion.11, s32[]{:T(128)S(6)} %select_n.28), kind=kOutput, calls=%fused_computation.1 | convolution fusion | flops 294912000 | bytes 14746116 | tf_op jit(solution)/shard_map/dot_general | solution.py:65
  186.5 0.0 copy-start.1
  186.6 5.3 %copy.13 = bf16[2,8,320,1152]{3,2,1,0:T(8,128)(2,1)} copy(bf16[2,8,320,1152]{3,1,2,0:T(8,128)(2,1)S(1)} %bitcast.21) | data formatting | bytes 23592960
  (1 shorter events, 0.0 us)
Async XLA Ops:
  7.2 2.1 %copy-start = (bf16[1,448,1280]{2,1,0:T(8,128)(2,1)S(1)}, bf16[1,448,1280]{2,1,0:T(8,128)(2,1)}, u32[]{:S(2)}) copy-start(bf16[1,448,1280]{2,1,0:T(8,128)(2,1)} %param.6) | copy-start | bytes 3440644
  7.2 72.5 %reduce-scatter.4.cloned.1.call-start = ((), (), s32[]{:S(2)}) async-start(), calls=%async_computation.4 | async-start | bytes 3686400 | tf_op jit(solution)/shard_map/reduce_scatter | solution.py:53
  19.4 122.4 %all-gather.4.cloned.1.call-start = ((), (), s32[]{:S(2)}) async-start(), calls=%async_computation.2 | async-start | bytes 3686400 | tf_op jit(solution)/shard_map/all_gather | solution.py:48
  19.5 13.7 %copy-start.3 = (f32[16,32]{1,0:T(8,128)S(1)}, f32[16,32]{1,0:T(8,128)}, u32[]{:S(2)}) copy-start(f32[16,32]{1,0:T(8,128)} %param.9) | copy-start | bytes 6148
  19.5 13.7 %copy-start.4 = (s32[4]{0:T(128)S(1)}, s32[4]{0:T(128)}, u32[]{:S(2)}) copy-start(s32[4]{0:T(128)} %param.10) | copy-start | bytes 52
  46.8 94.9 %copy-start.2 = (bf16[1,448,1152]{2,1,0:T(8,128)(2,1)S(1)}, bf16[1,448,1152]{2,1,0:T(8,128)(2,1)}, u32[]{:S(2)}) copy-start(bf16[1,448,1152]{2,1,0:T(8,128)(2,1)} %param.7) | copy-start | bytes 3096580
  70.5 98.9 %all-gather.6.cloned.1.call-start = ((), (), s32[]{:S(2)}) async-start(), calls=%async_computation.3 | async-start | bytes 3686400 | tf_op jit(solution)/shard_map/all_gather | solution.py:62
  186.5 5.3 %copy-start.1 = (bf16[1,448,1280]{2,1,0:T(8,128)(2,1)S(1)}, bf16[1,448,1280]{2,1,0:T(8,128)(2,1)}, u32[]{:S(2)}) copy-start(bf16[1,448,1280]{2,1,0:T(8,128)(2,1)} %param.6) | copy-start | bytes 3440644
Sparse Core Ops, SparseCore 0:
  19.5 60.0 reduce-scatter.3
  81.8 59.9 all-gather.3
  143.3 26.0 all-gather.5
where the time goes:
time: 199 us; the launch traced here: 198 us
  waiting for transfers between devices  94.3 us (47%)
  other arithmetic  30.4 us (15%)
  blocking collectives  22.3 us (11%)
  matrix products  22 us (11%)
  local copies, waits for them, and re-layouts  15.3 us (8%)
  between operations  13.8 us (7%)
    all_gather x1, waiting for transfers between devices, body(): lax.all_gather(merged_rows, 'edge', axis=0, tiled=True)  62.1 us
    all_gather x1, waiting for transfers between devices, body(): lax.all_gather(system_rows[None], ('expert', 'sys'), axis=0, tiled=True)  23.1 us
    all_to_all x1, blocking collectives, body(): lax.all_to_all(partials, 'expert', split_axis=0, concat_axis=0, tiled=True)  22.3 us
    convert_element_type x1, other arithmetic, body(): expert_weights.astype(jnp.float32)[None]  13.6 us
    reduce_sum x1, other arithmetic, body(): jnp.sum(own_coeffs[:, :, None, None] * expert_weights.astype(jnp.float32)...  13.5 us
    dot_general x1, matrix products, body(): folded = jnp.dot(local_coeffs, flat_rows, precision=highest)  12.6 us
    unnamed x12, local copies, waits for them, and re-layouts  10.7 us
    reduce_scatter x1, waiting for transfers between devices, body(): lax.psum_scatter(lax.dot_general(features, masked_grad, (((0,), (0,)), ((...  9.04 us
  transfers between devices with their start and end apart: 3, of which 3 were waited for; matrix products, arithmetic and copies ran while one was open for 17% of the time, Pallas kernels for 0%

commit v1 on v0

--- a/solution.py
+++ b/solution.py
@@ -59,7 +59,31 @@
         tiled=True,
     )
     local_coeffs = lax.dynamic_slice_in_dim(coeffs, expert_at * exp_local, exp_local, 1).T
-    block_rows = lax.all_gather(system_rows[None], ("expert", "sys"), axis=0, tiled=True)
+    peers, index, width = (
+        lax.axis_size(("expert", "sys")),
+        lax.axis_index(("expert", "sys")),
+        system_rows[None].shape[0],
+    )
+    right = [(i, (i + 1) % peers) for i in range(peers)]
+    backward = [(i, (i - 1) % peers) for i in range(peers)]
+    filled = jnp.zeros(
+        (*system_rows[None].shape[:0], peers * width, *system_rows[None].shape[0 + 1 :]),
+        system_rows[None].dtype,
+    )
+    filled = lax.dynamic_update_slice_in_dim(filled, system_rows[None], index * width, axis=0)
+    from_left = from_right = system_rows[None]
+    half = peers // 2
+    for step in range(1, half + 1):
+        from_left = lax.ppermute(from_left, ("expert", "sys"), right)
+        filled = lax.dynamic_update_slice_in_dim(
+            filled, from_left, (index - step) % peers * width, axis=0
+        )
+        if step < peers - half:
+            from_right = lax.ppermute(from_right, ("expert", "sys"), backward)
+            filled = lax.dynamic_update_slice_in_dim(
+                filled, from_right, (index + step) % peers * width, axis=0
+            )
+    block_rows = filled
     span_rows = block_rows.shape[0]
     flat_rows = block_rows.reshape(span_rows, -1).astype(jnp.float32)
     folded = jnp.dot(local_coeffs, flat_rows, precision=highest)

time: 199 us -> 184 us (0.925)
  waiting for transfers between devices: 94.3 us -> 77.4 us
    all_gather x1 -> x0, waiting for transfers between devices: 23.1 us -> none  [body(): lax.all_gather(system_rows[None], ('expert', 'sys'), axis=0, tiled=True)]
    ppermute x0 -> x3, waiting for transfers between devices: none -> 10.3 us  [the longest x2 10.3 us: body(): from_left = lax.ppermute(from_left, ('expert', 'sys'), right)]
    unnamed x3, waiting for transfers between devices: 0.05 us -> 9.34 us
    reduce_scatter x1 -> x0, waiting for transfers between devices: 9.04 us -> none  [body(): lax.psum_scatter(lax.dot_general(features, masked_grad, (((0,), (0,)), ((...]
    reshape x1 -> x0, local copies, waits for them, and re-layouts: 4.52 us -> none  [body(): flat_rows = block_rows.reshape(span_rows, -1).astype(jnp.float32)]
    all_gather x1, waiting for transfers between devices: 62.1 us -> 57.8 us  [body(): lax.all_gather(merged_rows, 'edge', axis=0, tiled=True)]
    unnamed x12, local copies, waits for them, and re-layouts: 10.7 us -> 14.7 us
  transfers between devices with their start and end apart: 3 -> 5, of which waited for: 3 -> 3; matrix products, arithmetic and copies ran while one was open for 17% -> 20% of each run, Pallas kernels for 0% -> 0%
where the time goes in v1:
time: 184 us; the launch traced here: 183 us
  waiting for transfers between devices  77.4 us (42%)
  other arithmetic  30.4 us (17%)
  blocking collectives  22.2 us (12%)
  matrix products  20.9 us (11%)
  local copies, waits for them, and re-layouts  16.2 us (9%)
  between operations  14.2 us (8%)
    all_gather x1, waiting for transfers between devices, body(): lax.all_gather(merged_rows, 'edge', axis=0, tiled=True)  57.8 us
    all_to_all x1, blocking collectives, body(): lax.all_to_all(partials, 'expert', split_axis=0, concat_axis=0, tiled=True)  22.2 us
    unnamed x12, local copies, waits for them, and re-layouts  14.7 us
    convert_element_type x1, other arithmetic, body(): expert_weights.astype(jnp.float32)[None]  13.6 us
    reduce_sum x1, other arithmetic, body(): jnp.sum(own_coeffs[:, :, None, None] * expert_weights.astype(jnp.float32)...  13.5 us
    dot_general x1, matrix products, body(): folded = jnp.dot(local_coeffs, flat_rows, precision=highest)  11.2 us
    ppermute x2, waiting for transfers between devices, body(): from_left = lax.ppermute(from_left, ('expert', 'sys'), right)  10.3 us
    unnamed x3, waiting for transfers between devices  9.34 us
  transfers between devices with their start and end apart: 5, of which 3 were waited for; matrix products, arithmetic and copies ran while one was open for 20% of the time, Pallas kernels for 0%

profile of v1, /device:TPU:0, one launch (start us, length us, event | category | flops | bytes accessed | tf_op | source)
XLA Modules:
  0.0 183.2 jit_solution(14726288306122678465)
XLA Ops:
  7.2 0.0 copy-start
  7.2 0.0 reduce-scatter.4.cloned.1.call-start
  7.2 1.4 fusion.14
  8.6 0.7 add_compare_fusion
  9.3 4.6 %fusion.1 = bf16[1280,1152]{0,1:T(8,128)(2,1)} fusion(bf16[1,448,1280]{2,1,0:T(8,128)(2,1)S(1)} %copy-done, bf16[1,448,1152]{2,1,0:T(8,128)(2,1)} %param.7, pred[448]{0:T(512)(128)(4,1)S(1)} %add_compare_fusion), kind=kOutput, calls=%fused_computation.4 | convolution fusion | flops 1323196416 | bytes 5128640 | tf_op jit(solution)/shard_map/dot_general | solution.py:54
  13.9 5.4 %copy.18 = bf16[1280,1152]{1,0:T(8,128)(2,1)} copy(bf16[1280,1152]{0,1:T(8,128)(2,1)} %fusion.1) | data formatting | bytes 5898240
  19.4 0.0 reduce-scatter.4.cloned.1.call-update
  19.4 0.0 all-gather.2.cloned.1.call-start
  19.4 0.0 copy-start.2
  19.5 13.6 %convert_element_type.25 = f32[16,320,1152]{2,1,0:T(8,128)} convert(bf16[16,320,1152]{2,1,0:T(8,128)(2,1)} %param.8) | non-fusion elementwise | flops 5898240 | bytes 35389440 | tf_op jit(solution)/shard_map/convert_element_type | solution.py:38
  33.1 0.2 fusion.11
  33.3 0.1 constant_dynamic-slice_fusion
  33.3 13.5 %multiply_reduce_fusion = bf16[2,320,1152]{2,1,0:T(8,128)(2,1)S(1)} fusion(f32[16,320,1152]{2,1,0:T(8,128)} %convert_element_type.25, f32[2,16]{1,0:T(2,128)S(1)} %bitcast.30), kind=kLoop, calls=%fused_computation.2 | loop fusion | flops 22855680 | bytes 25067648 | tf_op jit(solution)/shard_map/reduce_sum | solution.py:37
  46.8 22.2 %all_to_all.5 = bf16[2,320,1152]{2,1,0:T(8,128)(2,1)S(1)} all-to-all(bf16[2,320,1152]{2,1,0:T(8,128)(2,1)S(1)} %multiply_reduce_fusion), channel_id=1, replica_groups=mesh['groups'=2,'edge'=4,'expert'=2,'sys'=2] {'expert'}, dimensions={0} | all-to-all | bytes 2949120 | tf_op jit(solution)/shard_map/all_to_all | solution.py:41
  69.0 1.3 reduce_sum.32
  70.3 0.0 all-gather.2.cloned.1.call-update
  70.3 9.3 %reduce-scatter.4.cloned.1.call-done = bf16[320,1152]{1,0:T(8,128)(2,1)} async-done(((bf16[1280,1152]{1,0:T(8,128)(2,1)}), bf16[320,1152]{1,0:T(8,128)(2,1)}) %reduce-scatter.4.cloned.1.call-update) | async-done | bytes 737296
  79.6 1.7 copy.19
  81.4 0.8 copy.15
  82.2 0.1 collective-permute-start
  82.3 1.7 collective-permute-start.1
  84.0 57.8 %all-gather.2.cloned.1.call-done = bf16[1280,1152]{1,0:T(8,128)(2,1)} async-done(((bf16[320,1152]{1,0:T(8,128)(2,1)}), bf16[1280,1152]{1,0:T(8,128)(2,1)}) %all-gather.2.cloned.1.call-update) | async-done | bytes 2949136 | tf_op jit(solution)/shard_map/all_gather | solution.py:48
  141.8 4.9 %fusion.2 = bf16[1,448,1280]{2,1,0:T(8,128)(2,1)} fusion(bf16[1280,1152]{1,0:T(8,128)(2,1)} %all-gather.2.cloned.1.call-done, bf16[1,448,1152]{2,1,0:T(8,128)(2,1)} %param.7, pred[448]{0:T(512)(128)(4,1)S(1)} %add_compare_fusion), kind=kOutput, calls=%fused_computation.6 | convolution fusion | flops 1322295296 | bytes 5128640 | tf_op jit(solution)/shard_map/dot_general | solution.py:46
  146.6 0.2 broadcast_in_dim.39
  146.9 0.1 constant_dynamic-update-slice_fusion.3
  147.0 0.1 constant_dynamic-update-slice_fusion.2
  147.1 0.1 constant_dynamic-update-slice_fusion.1
  147.2 10.3 %collective-permute-done.2 = bf16[1,320,1152]{2,1,0:T(8,128)(2,1)S(1)} collective-permute-done((bf16[1,320,1152]{2,1,0:T(8,128)(2,1)S(1)}, bf16[1,320,1152]{2,1,0:T(8,128)(2,1)S(1)}, u32[]{:S(2)}, u32[]{:S(2)}) %collective-permute-start.2) | collective-permute-done | bytes 737312 | tf_op jit(solution)/shard_map/ppermute | solution.py:77
  157.5 0.1 constant_dynamic-update-slice_fusion
  157.6 2.3 %copy.20 = bf16[1,4,320,1152]{3,1,2,0:T(4,128)(2,1)S(1)} copy(bf16[1,4,320,1152]{3,2,1,0:T(8,128)(2,1)S(1)} %bitcast.27) | data formatting | bytes 5898240
  159.9 11.2 %fusion = bf16[16,368640]{1,0:T(8,128)(2,1)S(1)} fusion(bf16[4,368640]{1,0:T(4,128)(2,1)S(1)} %bitcast.25, f32[4,32]{1,0:T(4,128)S(1)} %fusion.11, s32[]{:T(128)S(6)} %select_n.55), kind=kOutput, calls=%fused_computation.1 | convolution fusion | flops 294912000 | bytes 14746116 | tf_op jit(solution)/shard_map/dot_general | solution.py:89
  171.1 5.3 %copy.21 = bf16[2,8,320,1152]{3,2,1,0:T(8,128)(2,1)} copy(bf16[2,8,320,1152]{3,1,2,0:T(8,128)(2,1)S(1)} %bitcast.24) | data formatting | bytes 23592960
  (9 shorter events, 0.0 us)
Async XLA Ops:
  7.2 2.1 %copy-start = (bf16[1,448,1280]{2,1,0:T(8,128)(2,1)S(1)}, bf16[1,448,1280]{2,1,0:T(8,128)(2,1)}, u32[]{:S(2)}) copy-start(bf16[1,448,1280]{2,1,0:T(8,128)(2,1)} %param.6) | copy-start | bytes 3440644
  7.2 72.5 %reduce-scatter.4.cloned.1.call-start = ((), (), s32[]{:S(2)}) async-start(), calls=%async_computation.3 | async-start | bytes 3686400
  19.4 122.4 %all-gather.2.cloned.1.call-start = ((), (), s32[]{:S(2)}) async-start(), calls=%async_computation.2 | async-start | bytes 3686400 | tf_op jit(solution)/shard_map/all_gather | solution.py:48
  19.4 13.6 %copy-start.2 = (f32[16,32]{1,0:T(8,128)S(1)}, f32[16,32]{1,0:T(8,128)}, u32[]{:S(2)}) copy-start(f32[16,32]{1,0:T(8,128)} %param.9) | copy-start | bytes 6148
  19.5 13.6 %copy-start.3 = (s32[4]{0:T(128)S(1)}, s32[4]{0:T(128)}, u32[]{:S(2)}) copy-start(s32[4]{0:T(128)} %param.10) | copy-start | bytes 52
  82.2 64.4 %collective-permute-start = (bf16[1,320,1152]{2,1,0:T(8,128)(2,1)S(1)}, bf16[1,320,1152]{2,1,0:T(8,128)(2,1)S(1)}, u32[]{:S(2)}, u32[]{:S(2)}) collective-permute-start(bf16[1,320,1152]{2,1,0:T(8,128)(2,1)S(1)} %copy.15), channel_id=1, source_target_pairs={{0,1},{1,2},{2,3},{3,0},{4,5},{5,6},{6,7},{7,4},{8,9},{9,10},{10,1... | collective-permute-start | bytes 2211848 | tf_op jit(solution)/shard_map/ppermute | solution.py:77
  82.3 64.8 %collective-permute-start.1 = (bf16[1,320,1152]{2,1,0:T(8,128)(2,1)S(1)}, bf16[1,320,1152]{2,1,0:T(8,128)(2,1)S(1)}, u32[]{:S(2)}, u32[]{:S(2)}) collective-permute-start(bf16[1,320,1152]{2,1,0:T(8,128)(2,1)S(1)} %copy.15), channel_id=1, source_target_pairs={{0,3},{1,0},{2,1},{3,2},{4,7},{5,4},{6,5},{7,6},{8,11},{9,8},{10,9... | collective-permute-start | bytes 2211848 | tf_op jit(solution)/shard_map/ppermute | solution.py:82
  146.6 10.9 %collective-permute-start.2 = (bf16[1,320,1152]{2,1,0:T(8,128)(2,1)S(1)}, bf16[1,320,1152]{2,1,0:T(8,128)(2,1)S(1)}, u32[]{:S(2)}, u32[]{:S(2)}) collective-permute-start(bf16[1,320,1152]{2,1,0:T(8,128)(2,1)S(1)} %collective-permute-done), channel_id=1, source_target_pairs={{0,1},{1,2},{2,3},{3,0},{4,5},{5,6},{6,7},{7,4},{8,9},{9,10},{10,1... | collective-permute-start | bytes 2211848 | tf_op jit(solution)/shard_map/ppermute | solution.py:77
  171.1 5.3 %copy-start.1 = (bf16[1,448,1280]{2,1,0:T(8,128)(2,1)S(1)}, bf16[1,448,1280]{2,1,0:T(8,128)(2,1)}, u32[]{:S(2)}) copy-start(bf16[1,448,1280]{2,1,0:T(8,128)(2,1)} %param.6) | copy-start | bytes 3440644
Sparse Core Ops, SparseCore 0:
  19.5 60.0 reduce-scatter.3
  81.8 59.9 all-gather.1
